TPU v7x, 32 devices: a whole 2x2x4 slice. The times are simulated.
32 devices in a mesh: ctx: 8 (over z, y), head: 4 (over x, core).
Axes of the slice: x: 2, y: 2, z: 4, core: 2. Of those that a mesh axis runs over, the one named last changes fastest.
Arguments:
- queries: bfloat16 [4096, 4096], P(('ctx', 'head')), may hold values from -6 to 6
- keys: bfloat16 [4096, 1024], P(('ctx', 'head')), may hold values from -6 to 6
- values: bfloat16 [4096, 1024], P(('ctx', 'head')), may hold values from -6 to 6
- cotangent: bfloat16 [4096, 4096], P(('ctx', 'head')), may hold values from -6 to 6
Outputs:
- out: bfloat16 [4096, 4096], P(('ctx', 'head'))
- grad_queries: bfloat16 [4096, 4096], P(('ctx', 'head'))
- grad_keys: bfloat16 [4096, 1024], P(('ctx', 'head'))
- grad_values: bfloat16 [4096, 1024], P(('ctx', 'head'))
All inputs are finite; a program needn't handle non-finite values.
Results may differ from a plain program's by a relative error of at most 0.008.
Values may be sent and summed in bfloat16 or wider, within the bound.
No kernel may reach another device: no remote copies, remote signals or barrier semaphores. Data moves between devices by JAX's collectives and lax.ppermute only.
A program may use at most 64 MiB of HBM per device.

v0:
```python
import jax
import jax.numpy as jnp
from jax import lax
from jax.sharding import PartitionSpec as P

QUERY_HEADS = 32
KEY_VALUE_HEADS = 8
HEAD_FEATURES = 128
BLOCK_POSITIONS = 512


LOWEST = -1e30


def from_behind(block, axis, distance):
    devices = range(lax.axis_size(axis))
    route = [(i - distance, i) for i in devices if i - distance in devices]
    return lax.ppermute(block, axis, route)


def head_terms(
    query, grad_out, band_keys, band_values, block_summary_keys, block_summary_values, first, keep
):
    row_count = query.shape[0]
    width = band_keys.shape[0]
    scale = query.shape[1] ** (-0.5)
    query_pos = first + jnp.arange(row_count, dtype=jnp.int32)
    key_pos = first - (width - row_count) + jnp.arange(width, dtype=jnp.int32)
    band_mask = (key_pos[None, :] >= 0) & (key_pos[None, :] <= query_pos[:, None])
    summary_mask = (
        jnp.arange(block_summary_keys.shape[0], dtype=jnp.int32)[None, :] < first // BLOCK_POSITIONS
    )
    band_score = jnp.dot(query, band_keys.T, preferred_element_type=jnp.float32) * scale
    summary_score = jnp.dot(query, block_summary_keys.T, preferred_element_type=jnp.float32) * scale
    row_top = jnp.maximum(
        jnp.max(jnp.where(band_mask, band_score, LOWEST), axis=1),
        jnp.max(jnp.where(summary_mask, summary_score, LOWEST), axis=1),
    )
    band_weight = jnp.where(band_mask, jnp.exp(band_score - row_top[:, None]), 0.0)
    summary_weight = jnp.where(summary_mask, jnp.exp(summary_score - row_top[:, None]), 0.0)
    row_total = jnp.sum(band_weight, axis=1) + jnp.sum(summary_weight, axis=1)
    band_prob = band_weight / row_total[:, None]
    summary_prob = summary_weight / row_total[:, None]
    band_low = band_prob.astype(jnp.bfloat16)
    summary_low = summary_prob.astype(jnp.bfloat16)
    attended = jnp.dot(band_low, band_values, preferred_element_type=jnp.float32) + jnp.dot(
        summary_low, block_summary_values, preferred_element_type=jnp.float32
    )
    row_dot = jnp.sum(grad_out.astype(jnp.float32) * attended, axis=1)
    band_back = jnp.dot(grad_out, band_values.T, preferred_element_type=jnp.float32)
    summary_back = jnp.dot(grad_out, block_summary_values.T, preferred_element_type=jnp.float32)
    band_slope = (band_prob * (band_back - row_dot[:, None])).astype(jnp.bfloat16)
    summary_slope = (summary_prob * (summary_back - row_dot[:, None])).astype(jnp.bfloat16)
    grad_query = (
        jnp.dot(band_slope, band_keys, preferred_element_type=jnp.float32)
        + jnp.dot(summary_slope, block_summary_keys, preferred_element_type=jnp.float32)
    ) * scale
    grad_key = jnp.dot(band_slope.T, query, preferred_element_type=jnp.float32) * scale
    grad_value = jnp.dot(band_low.T, grad_out, preferred_element_type=jnp.float32)
    grad_sum_key = jnp.dot(summary_slope.T, query, preferred_element_type=jnp.float32) * scale
    grad_sum_value = jnp.dot(summary_low.T, grad_out, preferred_element_type=jnp.float32)
    return (
        attended,
        grad_query,
        grad_key,
        grad_value,
        grad_sum_key,
        grad_sum_value,
        row_top,
        row_total,
        row_dot,
    )


def split_heads(block_rows, depth):
    return block_rows.reshape(block_rows.shape[0], -1, depth).transpose(1, 0, 2)


def merge_heads(head_rows, groups):
    number, row_count, depth = head_rows.shape
    return head_rows.transpose(1, 0, 2).reshape(row_count, groups, number // groups * depth)


def fold_heads(head_rows, groups):
    number, row_count, depth = head_rows.shape
    return (
        head_rows.reshape(groups, number // groups, row_count, depth).sum(axis=1).transpose(1, 0, 2)
    )


def repeat_heads(rows_first, head_count):
    return jnp.repeat(rows_first.transpose(1, 0, 2), head_count, axis=0)


def attend(query_x, key_x, value_x, grad_x):
    tokens, groups, depth = key_x.shape
    head_count = query_x.shape[2] // depth
    blocks = tokens // BLOCK_POSITIONS
    scaled = grad_x * 16
    edge_keys, edge_values = from_behind((key_x, value_x), "ctx", 1)
    pooled_keys = (
        jnp.sum(key_x.reshape(blocks, BLOCK_POSITIONS, groups, depth), axis=1, dtype=jnp.float32)
        / BLOCK_POSITIONS
    ).astype(jnp.bfloat16)
    pooled_values = (
        jnp.sum(value_x.reshape(blocks, BLOCK_POSITIONS, groups, depth), axis=1, dtype=jnp.float32)
        / BLOCK_POSITIONS
    ).astype(jnp.bfloat16)
    block_summary_keys, block_summary_values = (
        lax.all_gather(pooled_keys, "ctx", axis=0, tiled=True),
        lax.all_gather(pooled_values, "ctx", axis=0, tiled=True),
    )
    number = block_summary_keys.shape[0]
    summary_key_heads = repeat_heads(block_summary_keys, head_count)
    summary_value_heads = repeat_heads(block_summary_values, head_count)
    anchor = lax.axis_index("ctx") * tokens
    first_keep = 2 * BLOCK_POSITIONS
    key_grads = [jnp.zeros((BLOCK_POSITIONS, groups, depth), jnp.float32)]
    value_grads = [jnp.zeros((BLOCK_POSITIONS, groups, depth), jnp.float32)]
    block = 0
    lower = block * BLOCK_POSITIONS
    band_keys = jnp.concatenate([edge_keys, key_x], axis=0)
    band_values = jnp.concatenate([edge_values, value_x], axis=0)
    query_heads = split_heads(query_x, depth)
    grad_heads = split_heads(scaled, depth)
    first = anchor + lower
    term_list = lax.map(
        lambda items: head_terms(*items, first, first_keep),
        (
            query_heads,
            grad_heads,
            repeat_heads(band_keys, head_count),
            repeat_heads(band_values, head_count),
            summary_key_heads,
            summary_value_heads,
        ),
    )
    outputs = merge_heads(term_list[0], groups)
    query_grads = merge_heads(term_list[1], groups)
    local_key_gradient = fold_heads(term_list[2], groups)
    local_value_gradient = fold_heads(term_list[3], groups)
    key_grads[block] = local_key_gradient[first_keep - BLOCK_POSITIONS :]
    value_grads[block] = local_value_gradient[first_keep - BLOCK_POSITIONS :]
    edge_key_grad = local_key_gradient[:BLOCK_POSITIONS]
    edge_value_grad = local_value_gradient[:BLOCK_POSITIONS]
    summary_key_grad = term_list[4].reshape(groups, head_count, number, depth).sum(axis=1)
    summary_value_grad = term_list[5].reshape(groups, head_count, number, depth).sum(axis=1)
    later_keys, later_values = from_behind((edge_key_grad, edge_value_grad), "ctx", -1)
    key_grads[blocks - 1] = key_grads[blocks - 1] + later_keys
    value_grads[blocks - 1] = value_grads[blocks - 1] + later_values
    key_totals, value_totals = lax.psum((summary_key_grad, summary_value_grad), "ctx")
    start_offset = lax.axis_index("ctx") * blocks
    share_keys = lax.dynamic_slice_in_dim(key_totals, start_offset, blocks, 1)
    share_values = lax.dynamic_slice_in_dim(value_totals, start_offset, blocks, 1)
    block = 0
    key_grads[block] = key_grads[block] + share_keys[:, block, :][None] / BLOCK_POSITIONS
    value_grads[block] = value_grads[block] + share_values[:, block, :][None] / BLOCK_POSITIONS
    attended = outputs.astype(jnp.bfloat16)
    grad_queries = query_grads.astype(jnp.bfloat16)
    grad_keys = key_grads[0].astype(jnp.bfloat16)
    grad_values = value_grads[0].astype(jnp.bfloat16)
    return (attended, grad_queries, grad_keys, grad_values)


def finish(arrays):
    query_x, key_x, value_x, grad_x = arrays
    layer_outputs = attend(query_x[:, 0], key_x[:, 0], value_x[:, 0], grad_x[:, 0])
    return (
        lax.all_to_all(layer_outputs[0][:, None], "head", split_axis=0, concat_axis=1, tiled=True),
        lax.all_to_all(layer_outputs[1][:, None], "head", split_axis=0, concat_axis=1, tiled=True),
        lax.all_to_all(layer_outputs[2][:, None], "head", split_axis=0, concat_axis=1, tiled=True),
        lax.all_to_all(layer_outputs[3][:, None], "head", split_axis=0, concat_axis=1, tiled=True),
    )


def shards(queries, keys, values, cotangent):
    row_count = queries.shape[0]
    part_count = lax.axis_size("head")
    each_part_size = KEY_VALUE_HEADS // part_count
    head_count = QUERY_HEADS // KEY_VALUE_HEADS
    query_split = queries.reshape(row_count, part_count, each_part_size, head_count * HEAD_FEATURES)
    key_split = keys.reshape(row_count, part_count, each_part_size, HEAD_FEATURES)
    value_split = values.reshape(row_count, part_count, each_part_size, HEAD_FEATURES)
    grad_split = cotangent.reshape(
        row_count, part_count, each_part_size, head_count * HEAD_FEATURES
    )
    moved = (
        lax.all_to_all(query_split, "head", split_axis=1, concat_axis=0, tiled=True),
        lax.all_to_all(key_split, "head", split_axis=1, concat_axis=0, tiled=True),
        lax.all_to_all(value_split, "head", split_axis=1, concat_axis=0, tiled=True),
        lax.all_to_all(grad_split, "head", split_axis=1, concat_axis=0, tiled=True),
    )
    layer_outputs = finish(moved)
    return (
        layer_outputs[0].reshape(row_count, QUERY_HEADS * HEAD_FEATURES),
        layer_outputs[1].reshape(row_count, QUERY_HEADS * HEAD_FEATURES),
        layer_outputs[2].reshape(row_count, KEY_VALUE_HEADS * HEAD_FEATURES),
        layer_outputs[3].reshape(row_count, KEY_VALUE_HEADS * HEAD_FEATURES),
    )


def solution(mesh):
    placed = (
        P(("ctx", "head"), None),
        P(("ctx", "head"), None),
        P(("ctx", "head"), None),
        P(("ctx", "head"), None),
    )
    return jax.shard_map(
        shards,
        mesh=mesh,
        in_specs=placed,
        out_specs=(
            P(("ctx", "head"), None),
            P(("ctx", "head"), None),
            P(("ctx", "head"), None),
            P(("ctx", "head"), None),
        ),
        check_vma=False,
    )
```

profile of v0, /device:TPU:0, one launch (start us, length us, event | category | flops | bytes accessed | tf_op | source)
XLA Modules:
  0.0 362.9 jit_solution(3806091594254511671)
XLA Ops:
  0.6 1.9 copy.93
  2.5 4.2 %all-to-all-start.1 = ((bf16[128,4,2,128]{0,3,2,1:T(8,128)(2,1)}), bf16[128,4,2,128]{0,3,2,1:T(8,128)(2,1)S(1)}, u32[]{:S(2)}, u32[]{:S(2)}) async-start(bf16[128,4,2,128]{0,3,2,1:T(8,128)(2,1)} %bitcast.15), calls=%async_computation.1 | async-start | bytes 524288 | tf_op jit(solution)/shard_map/all_to_all | solution.py:189
  6.8 1.8 copy.96
  8.5 4.2 %all-to-all-done.1 = bf16[128,4,2,128]{0,3,2,1:T(8,128)(2,1)S(1)} async-done(((bf16[128,4,2,128]{0,3,2,1:T(8,128)(2,1)}), bf16[128,4,2,128]{0,3,2,1:T(8,128)(2,1)S(1)}, u32[]{:S(2)}, u32[]{:S(2)}) %all-to-all-start.1) | async-done | bytes 262176 | tf_op jit(solution)/shard_map/all_to_all | solution.py:189
  12.8 3.4 all-to-all-start.2
  17.0 1.8 copy.92
  18.8 3.4 all-to-all-done.2
  22.1 3.5 all-to-all-start
  27.2 12.9 %all-to-all-done = bf16[128,4,2,512]{3,2,0,1:T(2,128)(2,1)S(1)} async-done(((bf16[128,4,2,512]{3,2,0,1:T(2,128)(2,1)}), bf16[128,4,2,512]{3,2,0,1:T(2,128)(2,1)S(1)}, u32[]{:S(2)}, u32[]{:S(2)}) %all-to-all-start) | async-done | bytes 1048608 | tf_op jit(solution)/shard_map/all_to_all | solution.py:188
  40.1 3.5 all-to-all-start.3
  43.6 21.4 %all-gather.2 = bf16[8,2,128]{2,1,0:T(2,128)(2,1)S(1)} all-gather(bf16[1,2,128]{2,1,0:T(2,128)(2,1)S(1)} %fusion.69), channel_id=2, replica_groups=mesh['ctx'=8,'head'=4] {'ctx'}, dimensions={0}, use_global_device_ids=true | all-gather | bytes 4608 | tf_op jit(solution)/shard_map/all_gather | solution.py:110
  66.7 2.8 collective-permute-start
  69.6 17.7 %all-gather.3 = bf16[8,2,128]{2,1,0:T(2,128)(2,1)S(1)} all-gather(bf16[1,2,128]{2,1,0:T(2,128)(2,1)S(1)} %fusion.70), channel_id=3, replica_groups=mesh['ctx'=8,'head'=4] {'ctx'}, dimensions={0}, use_global_device_ids=true | all-gather | bytes 4608 | tf_op jit(solution)/shard_map/all_gather | solution.py:111
  92.7 1.5 copy.103
  94.2 1.7 broadcast_in_dim.110
  95.9 1.6 broadcast_in_dim.112
  97.5 155.8 %while.23 = (s32[]{:T(128)}, bf16[8,512,128]{1,2,0:T(8,128)(2,1)}, bf16[8,512,128]{1,2,0:T(8,128)(2,1)}, f32[8,1024,128]{2,1,0:T(8,128)}, f32[8,1024,128]{2,1,0:...) while((s32[]{:T(128)}, bf16[8,512,128]{1,2,0:T(8,128)(2,1)}, ...), condition=%wide.region_8.9_spmd, body=%wide.region_2.8_spmd.sunk | while | flops 823806976 | bytes 23803096 | solution.py:127
  98.6 1.8 select_reduce_fusion.4
  108.6 1.5 multiply_convert_fusion.4
  112.6 2.2 fusion.130
  114.7 2.2 fusion.129
  118.0 1.8 select_reduce_fusion.4
  122.7 1.4 fusion.125
  128.1 1.5 multiply_convert_fusion.4
  132.0 2.2 fusion.130
  134.2 2.2 fusion.129
  137.5 1.8 select_reduce_fusion.4
  142.2 1.4 fusion.125
  147.6 1.5 multiply_convert_fusion.4
  151.5 2.2 fusion.130
  153.7 2.2 fusion.129
  157.0 1.8 select_reduce_fusion.4
  167.1 1.5 multiply_convert_fusion.4
  171.0 2.2 fusion.130
  173.2 2.2 fusion.129
  176.5 1.8 select_reduce_fusion.4
  186.5 1.5 multiply_convert_fusion.4
  190.5 2.2 fusion.130
  192.7 2.2 fusion.129
  195.9 1.8 select_reduce_fusion.4
  200.6 1.4 fusion.125
  206.0 1.5 multiply_convert_fusion.4
  210.0 2.2 fusion.130
  212.1 2.2 fusion.129
  215.4 1.8 select_reduce_fusion.4
  225.5 1.5 multiply_convert_fusion.4
  229.4 2.2 fusion.130
  231.6 2.2 fusion.129
  234.9 1.8 select_reduce_fusion.4
  244.9 1.5 multiply_convert_fusion.4
  248.9 2.2 fusion.130
  251.0 2.2 fusion.129
  253.2 4.2 %bitcast_reduce_fusion = (f32[2,1024,128]{2,1,0:T(8,128)S(1)}, f32[2,1024,128]{2,1,0:T(8,128)S(1)}) fusion(f32[8,1024,128]{2,1,0:T(8,128)} %get-tuple-element.275, f32[8,1024,128]{2,1,0:T(8,128)} %get-tuple-element.273), kind=kLoop, calls=%fused_computation.80 | loop fusion | flops 1572864 | bytes 10485760 | tf_op jit(solution)/shard_map/reduce_sum | solution.py:87
  261.7 43.4 %all-reduce = (f32[2,8,128]{2,1,0:T(8,128)S(1)}, f32[2,8,128]{2,1,0:T(8,128)S(1)}) all-reduce(f32[2,8,128]{2,1,0:T(8,128)S(1)} %get-tuple-element.432, f32[2,8,128]{2,1,0:T(8,128)S(1)} %get-tuple-element.431), channel_id=1, replica_groups=mesh['ctx'=8,'head'=4] {'ctx'}, use_global_device_ids=true, to_apply=%region_11.12 | all-reduce | flops 4096 | bytes 32768 | tf_op jit(solution)/shard_map/psum | solution.py:151
  306.2 3.6 all-to-all-start.7
  310.8 4.7 %all-to-all-done.7 = bf16[512,1,2,128]{3,2,1,0:T(2,128)(2,1)S(1)} async-done(((bf16[512,1,2,128]{3,2,1,0:T(2,128)(2,1)}), bf16[512,1,2,128]{3,2,1,0:T(2,128)(2,1)S(1)}, u32[]{:S(2)}, u32[]{:S(2)}) %all-to-all-start.7) | async-done | bytes 262176 | tf_op jit(solution)/shard_map/all_to_all | solution.py:172
  315.6 3.4 all-to-all-start.6
  319.0 3.7 %copy.104 = bf16[512,1,2,512]{3,2,1,0:T(2,128)(2,1)} copy(bf16[512,1,2,512]{0,3,2,1:T(8,128)(2,1)} %bitcast.40) | data formatting | bytes 2097152 | tf_op jit(solution)/shard_map/convert_element_type | solution.py:158
  322.7 2.2 all-to-all-done.6
  324.9 3.5 all-to-all-start.4
  328.5 2.1 copy.108
  330.6 12.3 %all-to-all-done.4 = bf16[512,1,2,512]{3,2,1,0:T(2,128)(2,1)S(1)} async-done(((bf16[512,1,2,512]{3,2,1,0:T(2,128)(2,1)}), bf16[512,1,2,512]{3,2,1,0:T(2,128)(2,1)S(1)}, u32[]{:S(2)}, u32[]{:S(2)}) %all-to-all-start.4) | async-done | bytes 1048608 | tf_op jit(solution)/shard_map/all_to_all | solution.py:169
  342.9 3.5 all-to-all-start.5
  350.7 10.1 %all-to-all-done.5 = bf16[512,1,2,512]{3,2,1,0:T(2,128)(2,1)S(1)} async-done(((bf16[512,1,2,512]{3,2,1,0:T(2,128)(2,1)}), bf16[512,1,2,512]{3,2,1,0:T(2,128)(2,1)S(1)}, u32[]{:S(2)}, u32[]{:S(2)}) %all-to-all-start.5) | async-done | bytes 1048608 | tf_op jit(solution)/shard_map/all_to_all | solution.py:170
  (221 shorter events, 112.0 us)
Async XLA Ops:
  0.6 15.5 %copy-start.2 = (bf16[128,4096]{1,0:T(8,128)(2,1)S(1)}, bf16[128,4096]{1,0:T(8,128)(2,1)}, u32[]{:S(2)}) copy-start(bf16[128,4096]{1,0:T(8,128)(2,1)} %param.6) | copy-start | bytes 3145732
  2.5 10.2 %all-to-all-start.1 = ((bf16[128,4,2,128]{0,3,2,1:T(8,128)(2,1)}), bf16[128,4,2,128]{0,3,2,1:T(8,128)(2,1)S(1)}, u32[]{:S(2)}, u32[]{:S(2)}) async-start(bf16[128,4,2,128]{0,3,2,1:T(8,128)(2,1)} %bitcast.15), calls=%async_computation.1 | async-start | bytes 524288 | tf_op jit(solution)/shard_map/all_to_all | solution.py:189
  12.8 9.4 %all-to-all-start.2 = ((bf16[128,4,2,128]{0,3,2,1:T(8,128)(2,1)}), bf16[128,4,2,128]{0,3,2,1:T(8,128)(2,1)S(1)}, u32[]{:S(2)}, u32[]{:S(2)}) async-start(bf16[128,4,2,128]{0,3,2,1:T(8,128)(2,1)} %bitcast.25), calls=%async_computation.2 | async-start | bytes 524288 | tf_op jit(solution)/shard_map/all_to_all | solution.py:190
  17.0 8.8 %copy-start.3 = (bf16[128,4096]{1,0:T(8,128)(2,1)S(1)}, bf16[128,4096]{1,0:T(8,128)(2,1)}, u32[]{:S(2)}) copy-start(bf16[128,4096]{1,0:T(8,128)(2,1)} %param.9) | copy-start | bytes 3145732
  22.1 17.9 %all-to-all-start = ((bf16[128,4,2,512]{3,2,0,1:T(2,128)(2,1)}), bf16[128,4,2,512]{3,2,0,1:T(2,128)(2,1)S(1)}, u32[]{:S(2)}, u32[]{:S(2)}) async-start(bf16[128,4,2,512]{3,2,0,1:T(2,128)(2,1)} %copy.92), calls=%async_computation | async-start | bytes 2097152 | tf_op jit(solution)/shard_map/all_to_all | solution.py:188
  40.1 51.0 %all-to-all-start.3 = ((bf16[128,4,2,512]{0,3,2,1:T(8,128)(2,1)}), bf16[128,4,2,512]{0,3,2,1:T(8,128)(2,1)S(1)}, u32[]{:S(2)}, u32[]{:S(2)}) async-start(bf16[128,4,2,512]{0,3,2,1:T(8,128)(2,1)} %bitcast.35), calls=%async_computation.3 | async-start | bytes 2097152 | tf_op jit(solution)/shard_map/all_to_all | solution.py:191
  65.4 21.9 %collective-permute-start.1 = (bf16[512,2,128]{2,0,1:T(8,128)(2,1)S(1)}, bf16[512,2,128]{2,0,1:T(8,128)(2,1)S(1)}, u32[]{:S(2)}, u32[]{:S(2)}) collective-permute-start(bf16[512,2,128]{2,0,1:T(8,128)(2,1)S(1)} %bitcast.224), channel_id=1, source_target_pairs={{0,4},{4,8},{8,12},{12,16},{16,20},{20,24},{24,28},{1,5},{5,9},{9,... | collective-permute-start | bytes 786440 | tf_op jit(solution)/shard_map/ppermute | solution.py:18
  66.7 21.5 %collective-permute-start = (bf16[512,2,128]{2,0,1:T(8,128)(2,1)S(1)}, bf16[512,2,128]{2,0,1:T(8,128)(2,1)S(1)}, u32[]{:S(2)}, u32[]{:S(2)}) collective-permute-start(bf16[512,2,128]{2,0,1:T(8,128)(2,1)S(1)} %bitcast.222), channel_id=1, source_target_pairs={{0,4},{4,8},{8,12},{12,16},{16,20},{20,24},{24,28},{1,5},{5,9},{9,... | collective-permute-start | bytes 786440 | tf_op jit(solution)/shard_map/ppermute | solution.py:18
  92.0 2.2 copy-start.1
  92.7 3.2 copy-start
  258.3 46.8 %collective-permute-start.3 = (f32[512,2,128]{2,0,1:T(8,128)}, f32[512,2,128]{2,0,1:T(8,128)S(1)}, u32[]{:S(2)}, u32[]{:S(2)}) collective-permute-start(f32[512,2,128]{2,0,1:T(8,128)} %slice.19), channel_id=1, source_target_pairs={{4,0},{8,4},{12,8},{16,12},{20,16},{24,20},{28,24},{5,1},{9,5},{13... | collective-permute-start | bytes 1572872 | tf_op jit(solution)/shard_map/ppermute | solution.py:18
  260.4 49.4 %collective-permute-start.2 = (f32[512,2,128]{2,0,1:T(8,128)}, f32[512,2,128]{2,0,1:T(8,128)S(1)}, u32[]{:S(2)}, u32[]{:S(2)}) collective-permute-start(f32[512,2,128]{2,0,1:T(8,128)} %slice.17), channel_id=1, source_target_pairs={{4,0},{8,4},{12,8},{16,12},{20,16},{24,20},{28,24},{5,1},{9,5},{13... | collective-permute-start | bytes 1572872 | tf_op jit(solution)/shard_map/ppermute | solution.py:18
  306.2 9.4 %all-to-all-start.7 = ((bf16[512,1,2,128]{3,2,1,0:T(2,128)(2,1)}), bf16[512,1,2,128]{3,2,1,0:T(2,128)(2,1)S(1)}, u32[]{:S(2)}, u32[]{:S(2)}) async-start(bf16[512,1,2,128]{3,2,1,0:T(2,128)(2,1)} %copy.114), calls=%async_computation.7 | async-start | bytes 524288 | tf_op jit(solution)/shard_map/all_to_all | solution.py:172
  315.6 9.4 %all-to-all-start.6 = ((bf16[512,1,2,128]{3,2,1,0:T(2,128)(2,1)}), bf16[512,1,2,128]{3,2,1,0:T(2,128)(2,1)S(1)}, u32[]{:S(2)}, u32[]{:S(2)}) async-start(bf16[512,1,2,128]{3,2,1,0:T(2,128)(2,1)} %copy.111), calls=%async_computation.6 | async-start | bytes 524288 | tf_op jit(solution)/shard_map/all_to_all | solution.py:171
  319.0 9.5 %copy-start.4 = (bf16[8,512,128]{1,2,0:T(8,128)(2,1)S(1)}, bf16[8,512,128]{1,2,0:T(8,128)(2,1)}, u32[]{:S(2)}) copy-start(bf16[8,512,128]{1,2,0:T(8,128)(2,1)} %get-tuple-element.272) | copy-start | bytes 3145732
  324.9 17.9 %all-to-all-start.4 = ((bf16[512,1,2,512]{3,2,1,0:T(2,128)(2,1)}), bf16[512,1,2,512]{3,2,1,0:T(2,128)(2,1)S(1)}, u32[]{:S(2)}, u32[]{:S(2)}) async-start(bf16[512,1,2,512]{3,2,1,0:T(2,128)(2,1)} %copy.104), calls=%async_computation.4 | async-start | bytes 2097152 | tf_op jit(solution)/shard_map/all_to_all | solution.py:169
  342.9 17.9 %all-to-all-start.5 = ((bf16[512,1,2,512]{3,2,1,0:T(2,128)(2,1)}), bf16[512,1,2,512]{3,2,1,0:T(2,128)(2,1)S(1)}, u32[]{:S(2)}, u32[]{:S(2)}) async-start(bf16[512,1,2,512]{3,2,1,0:T(2,128)(2,1)} %copy.108), calls=%async_computation.5 | async-start | bytes 2097152 | tf_op jit(solution)/shard_map/all_to_all | solution.py:170
where the time goes:
time: 366 us; the launch traced here: 363 us
  matrix products  127 us (35%)
  blocking collectives  82.6 us (23%)
  waiting for transfers between devices  49.8 us (14%)
  local copies, waits for them, and re-layouts  38.3 us (10%)
  starting transfers between devices  35.3 us (10%)
  other arithmetic  28.6 us (8%)
    psum x1, blocking collectives, attend(): lax.psum((summary_key_grad, summary_value_grad), 'ctx')  43.4 us
    all_gather x1, blocking collectives, attend(): lax.all_gather(pooled_keys, 'ctx', axis=0, tiled=True)  21.4 us
    all_gather x1, blocking collectives, attend(): lax.all_gather(pooled_values, 'ctx', axis=0, tiled=True)  17.7 us
    dot_general x8, matrix products, head_terms(): jnp.dot(band_low.T, grad_out, preferred_element_type=jnp.float32)  17.4 us
    dot_general x8, matrix products, head_terms(): jnp.dot(band_slope.T, query, preferred_element_type=jnp.float32) * scale  17.4 us
    dot_general x8, matrix products, head_terms(): jnp.dot(query, band_keys.T, preferred_element_type=jnp.float32) * scale  14.2 us
    all_to_all x1, waiting for transfers between devices, shards(): lax.all_to_all(query_split, 'head', split_axis=1, concat_axis=0, tiled=True)  12.9 us
    all_to_all x1, waiting for transfers between devices, finish(): lax.all_to_all(layer_outputs[0][:, None], 'head', split_axis=0, concat_ax...  12.3 us
  transfers between devices with their start and end apart: 12, of which 7 were waited for; matrix products, arithmetic and copies ran while one was open for 6% of the time, Pallas kernels for 0%

commit v1 on v0

v1 whole, which is shorter than its diff:
```python
import jax
import jax.numpy as jnp
from jax import lax
from jax.experimental import pallas as pl
from jax.experimental.pallas import tpu as pltpu
from jax.sharding import PartitionSpec as P

QUERY_HEADS = 32
KEY_VALUE_HEADS = 8
DEPTH = 128
BLOCK = 512
TILE = 256
GROUP = QUERY_HEADS // KEY_VALUE_HEADS
LOWEST = -1e30
LOG2E = 1.4426950408889634

BF = jnp.bfloat16
F32 = jnp.float32


def dot(a, b, ca, cb):
    return lax.dot_general(a, b, (((ca,), (cb,)), ((), ())), preferred_element_type=F32)


def pack_kernel(q_ref, k_ref, v_ref, g_ref, kv_ref, a_ref, b_ref, s_ref):
    half = GROUP * DEPTH
    kv_ref[0, :, : 2 * DEPTH] = k_ref[...]
    kv_ref[0, :, 2 * DEPTH :] = v_ref[...]
    a_ref[0, :, :half] = q_ref[:, :half]
    a_ref[0, :, half:] = g_ref[:, :half]
    b_ref[0, :, :half] = q_ref[:, half:]
    b_ref[0, :, half:] = g_ref[:, half:]
    s_ref[0, :, : 2 * DEPTH] = jnp.sum(k_ref[...].astype(F32), axis=0, keepdims=True)
    s_ref[0, :, 2 * DEPTH :] = jnp.sum(v_ref[...].astype(F32), axis=0, keepdims=True)


def pack(q, k, v, g, parts):
    rows = q.shape[0]
    wide = 2 * GROUP * DEPTH
    return pl.pallas_call(
        pack_kernel,
        grid=(parts,),
        in_specs=[
            pl.BlockSpec((rows, wide), lambda i: (0, i)),
            pl.BlockSpec((rows, 2 * DEPTH), lambda i: (0, i)),
            pl.BlockSpec((rows, 2 * DEPTH), lambda i: (0, i)),
            pl.BlockSpec((rows, wide), lambda i: (0, i)),
        ],
        out_specs=[
            pl.BlockSpec((1, rows, 4 * DEPTH), lambda i: (i, 0, 0)),
            pl.BlockSpec((1, rows, wide), lambda i: (i, 0, 0)),
            pl.BlockSpec((1, rows, wide), lambda i: (i, 0, 0)),
            pl.BlockSpec((1, 1, 4 * DEPTH), lambda i: (i, 0, 0)),
        ],
        out_shape=[
            jax.ShapeDtypeStruct((parts, rows, 4 * DEPTH), BF),
            jax.ShapeDtypeStruct((parts, rows, wide), BF),
            jax.ShapeDtypeStruct((parts, rows, wide), BF),
            jax.ShapeDtypeStruct((parts, 1, 4 * DEPTH), F32),
        ],
        name="pack",
    )(q, k, v, g)


def attend_kernel(
    q_ref, g_ref, k_ref, v_ref, pk_ref, pv_ref, sk_ref, sv_ref,
    o_ref, dq_ref, edge_ref, own_ref, ds_ref,
    kc, vc, kt, vt, dk, dv,
):
    ctx = lax.axis_index("ctx")
    scale = DEPTH ** (-0.5)
    coef = scale * LOG2E
    count = sk_ref.shape[0]
    pad = kc.shape[0] - 2 * BLOCK
    head = pl.program_id(0)

    @pl.when(head == 0)
    def _():
        for ref, all_ref, own, prev, tr in (
            (sk_ref, kc, k_ref, pk_ref, kt),
            (sv_ref, vc, v_ref, pv_ref, vt),
        ):
            mean = (jnp.sum(ref[...], axis=1) * (1.0 / BLOCK)).astype(BF)
            if pad > count:
                mean = jnp.concatenate([mean, jnp.zeros((pad - count, DEPTH), BF)], axis=0)
            all_ref[:pad] = mean
            all_ref[pad : pad + BLOCK] = prev[...]
            all_ref[pad + BLOCK :] = own[...]
            tr[...] = all_ref[...].T
        dk[...] = jnp.zeros_like(dk)
        dv[...] = jnp.zeros_like(dv)

    for tile in range(BLOCK // TILE):
        rows = pl.ds(tile * TILE, TILE)
        edge = pad + BLOCK + TILE * (tile + 1)
        q = q_ref[rows, :]
        s = dot(kc[:edge], q, 1, 1)
        s_sum = s[:pad]
        s_prev = s[pad : pad + BLOCK]
        s_diag = s[edge - TILE :]
        at = lax.broadcasted_iota(jnp.int32, (pad, TILE), 0)
        s_sum = jnp.where(at < ctx, s_sum, LOWEST)
        ki = lax.broadcasted_iota(jnp.int32, (TILE, TILE), 0)
        qi = lax.broadcasted_iota(jnp.int32, (TILE, TILE), 1)
        s_diag = jnp.where(ki <= qi, s_diag, LOWEST)
        pieces = [s_sum, s_prev, s_diag]
        if tile > 0:
            pieces.insert(2, s[pad + BLOCK : edge - TILE])
        tops = [jnp.max(x, axis=0, keepdims=True) for x in pieces]
        tops[1] = jnp.where(ctx > 0, tops[1], LOWEST)
        top = tops[0]
        for x in tops[1:]:
            top = jnp.maximum(top, x)
        shift = [top] * len(pieces)
        shift[1] = jnp.where(ctx > 0, top, -LOWEST)
        weights = [jnp.exp2((x - y) * coef) for x, y in zip(pieces, shift)]
        total = sum(jnp.sum(x, axis=0, keepdims=True) for x in weights)
        inv = 1.0 / total
        weight = jnp.concatenate(weights, axis=0)
        low = weight.astype(BF)
        attended = dot(vt[:, :edge], low, 1, 0) * inv
        o_ref[rows, :] = attended.T.astype(BF)
        gt = (g_ref[rows, :].astype(F32).T * (16.0 * inv)).astype(BF)
        row_dot = jnp.sum(gt.astype(F32) * attended, axis=0, keepdims=True)
        back = dot(vc[:edge], gt, 1, 0)
        slope = (weight * (back - row_dot)).astype(BF)
        dq_ref[rows, :] = (dot(kt[:, :edge], slope, 1, 0) * scale).T.astype(BF)
        dk[:edge] += dot(slope, q, 1, 0)
        dv[:edge] += dot(low, gt, 1, 1)

    @pl.when(head == pl.num_programs(0) - 1)
    def _():
        ds_ref[:, :DEPTH] = dk[:count] * scale
        ds_ref[:, DEPTH:] = dv[:count]
        edge_ref[:, :DEPTH] = (dk[pad : pad + BLOCK] * scale).astype(BF)
        edge_ref[:, DEPTH:] = dv[pad : pad + BLOCK].astype(BF)
        own_ref[:, :DEPTH] = dk[pad + BLOCK :] * scale
        own_ref[:, DEPTH:] = dv[pad + BLOCK :]


def attend(qg, kv, prev, sums, which):
    count = sums.shape[0]
    pad = max(16, -(-count // 16) * 16)
    width = pad + 2 * BLOCK

    def column(col, moving=False):
        if moving:
            return pl.BlockSpec((BLOCK, DEPTH), lambda h: (0, h + col))
        return pl.BlockSpec((BLOCK, DEPTH), lambda h: (0, col))

    def summary(col):
        return pl.BlockSpec((count, sums.shape[1], DEPTH), lambda h: (0, 0, col))

    whole = lambda shape: pl.BlockSpec(shape, lambda h: (0, 0))
    outs = pl.pallas_call(
        attend_kernel,
        grid=(GROUP,),
        in_specs=[
            column(0, True),
            column(GROUP, True),
            column(which),
            column(2 + which),
            column(which),
            column(2 + which),
            summary(which),
            summary(2 + which),
        ],
        out_specs=[
            pl.BlockSpec((BLOCK, DEPTH), lambda h: (0, h)),
            pl.BlockSpec((BLOCK, DEPTH), lambda h: (0, h)),
            whole((BLOCK, 2 * DEPTH)),
            whole((BLOCK, 2 * DEPTH)),
            whole((count, 2 * DEPTH)),
        ],
        out_shape=[
            jax.ShapeDtypeStruct((BLOCK, GROUP * DEPTH), BF),
            jax.ShapeDtypeStruct((BLOCK, GROUP * DEPTH), BF),
            jax.ShapeDtypeStruct((BLOCK, 2 * DEPTH), BF),
            jax.ShapeDtypeStruct((BLOCK, 2 * DEPTH), F32),
            jax.ShapeDtypeStruct((count, 2 * DEPTH), F32),
        ],
        scratch_shapes=[
            pltpu.VMEM((width, DEPTH), BF),
            pltpu.VMEM((width, DEPTH), BF),
            pltpu.VMEM((DEPTH, width), BF),
            pltpu.VMEM((DEPTH, width), BF),
            pltpu.VMEM((width, DEPTH), F32),
            pltpu.VMEM((width, DEPTH), F32),
        ],
        cost_estimate=pl.CostEstimate(
            flops=12 * GROUP * BLOCK * 2 * BLOCK * DEPTH,
            bytes_accessed=8 * BLOCK * GROUP * DEPTH,
            transcendentals=GROUP * BLOCK * 2 * BLOCK,
        ),
        name="attend",
    )(qg, qg, kv, kv, prev, prev, sums, sums)
    return outs


def join_kernel(own_a, own_b, edge_a, edge_b, ds_ref, out_ref):
    total = jnp.sum(ds_ref[...], axis=0, keepdims=True) * (1.0 / BLOCK)
    for g, (own, edge) in enumerate(((own_a, edge_a), (own_b, edge_b))):
        both = own[...] + edge[...].astype(F32)
        for part in range(2):
            cols = slice(part * DEPTH, (part + 1) * DEPTH)
            spread = total[:, (2 * g + part) * DEPTH : (2 * g + part + 1) * DEPTH]
            at = (2 * part + g) * DEPTH
            out_ref[:, at : at + DEPTH] = (both[:, cols] + spread).astype(BF)


def join(own, edge, ds):
    return pl.pallas_call(
        join_kernel,
        out_shape=jax.ShapeDtypeStruct((BLOCK, 4 * DEPTH), BF),
        name="join",
    )(own[0], own[1], edge[0], edge[1], ds)


def unpack_kernel(oa_ref, qa_ref, ob_ref, qb_ref, kv_ref, o_ref, dq_ref, dk_ref, dv_ref):
    half = GROUP * DEPTH
    o_ref[:, :half] = oa_ref[0]
    o_ref[:, half:] = ob_ref[0]
    dq_ref[:, :half] = qa_ref[0]
    dq_ref[:, half:] = qb_ref[0]
    dk_ref[...] = kv_ref[0, :, : 2 * DEPTH]
    dv_ref[...] = kv_ref[0, :, 2 * DEPTH :]


def unpack(oa, qa, ob, qb, kv):
    parts, rows, half = oa.shape
    wide = pl.BlockSpec((1, rows, half), lambda i: (i, 0, 0))
    return pl.pallas_call(
        unpack_kernel,
        grid=(parts,),
        in_specs=[wide, wide, wide, wide, pl.BlockSpec((1, rows, 4 * DEPTH), lambda i: (i, 0, 0))],
        out_specs=[
            pl.BlockSpec((rows, 2 * half), lambda i: (0, i)),
            pl.BlockSpec((rows, 2 * half), lambda i: (0, i)),
            pl.BlockSpec((rows, 2 * DEPTH), lambda i: (0, i)),
            pl.BlockSpec((rows, 2 * DEPTH), lambda i: (0, i)),
        ],
        out_shape=[
            jax.ShapeDtypeStruct((rows, parts * 2 * half), BF),
            jax.ShapeDtypeStruct((rows, parts * 2 * half), BF),
            jax.ShapeDtypeStruct((rows, parts * 2 * DEPTH), BF),
            jax.ShapeDtypeStruct((rows, parts * 2 * DEPTH), BF),
        ],
        name="unpack",
    )(oa, qa, ob, qb, kv)


def exchange(x):
    return lax.all_to_all(x, "head", split_axis=0, concat_axis=0, tiled=True)


def shards(queries, keys, values, cotangent):
    rows = queries.shape[0]
    parts = lax.axis_size("head")
    blocks = lax.axis_size("ctx")
    assert rows * parts == BLOCK and parts * 2 == KEY_VALUE_HEADS
    kv, qg_a, qg_b, sums = pack(queries, keys, values, cotangent, parts)
    kv = exchange(kv).reshape(BLOCK, 4 * DEPTH)
    qg_a = exchange(qg_a).reshape(BLOCK, 2 * GROUP * DEPTH)
    qg_b = exchange(qg_b).reshape(BLOCK, 2 * GROUP * DEPTH)
    prev = lax.ppermute(kv, "ctx", [(i, i + 1) for i in range(blocks - 1)])
    sums = jnp.broadcast_to(sums.reshape(1, parts, 4 * DEPTH), (blocks, parts, 4 * DEPTH))
    sums = lax.all_to_all(
        sums.reshape(blocks * parts, 4 * DEPTH), ("ctx", "head"), 0, 0, tiled=True
    ).reshape(blocks, parts, 4 * DEPTH)
    o_a, q_a, edge_a, own_a, ds_a = attend(qg_a, kv, prev, sums, 0)
    o_b, q_b, edge_b, own_b, ds_b = attend(qg_b, kv, prev, sums, 1)
    back = [(i + 1, i) for i in range(blocks - 1)]
    edge_a = lax.ppermute(edge_a, "ctx", back)
    edge_b = lax.ppermute(edge_b, "ctx", back)
    ds = lax.all_to_all(jnp.concatenate([ds_a, ds_b], axis=1), "ctx", 0, 0, tiled=True)
    split = lambda x: x.reshape(parts, rows, x.shape[1])
    dkv = exchange(split(join((own_a, own_b), (edge_a, edge_b), ds)))
    return tuple(
        unpack(
            exchange(split(o_a)), exchange(split(q_a)),
            exchange(split(o_b)), exchange(split(q_b)), dkv,
        )
    )


def solution(mesh):
    placed = P(("ctx", "head"), None)
    return jax.shard_map(
        shards, mesh=mesh, in_specs=(placed,) * 4, out_specs=(placed,) * 4, check_vma=False
    )
```

time: 366 us -> 172 us (0.47)
  matrix products: 127 us -> 0 us
  Pallas kernels: 0 us -> 38.1 us
  local copies, waits for them, and re-layouts: 38.3 us -> 5.54 us
  other arithmetic: 28.6 us -> 0.86 us
  waiting for transfers between devices: 49.8 us -> 24.8 us
  starting transfers between devices: 35.3 us -> 15.8 us
    dot_general x96 -> x0, matrix products: 127 us -> none  [the longest x8 17.4 us: head_terms(): jnp.dot(band_low.T, grad_out, preferred_element_type=jnp.float32)]
    all_to_all x0 -> x7, blocking collectives: none -> 84.8 us  [the longest x5 61.3 us: exchange(): return lax.all_to_all(x, 'head', split_axis=0, concat_axis=0, tiled=True)]
    psum x1 -> x0, blocking collectives: 43.4 us -> none  [attend(): lax.psum((summary_key_grad, summary_value_grad), 'ctx')]
    all_gather x2 -> x0, blocking collectives: 39.2 us -> none  [the longest x1 21.4 us: attend(): lax.all_gather(pooled_keys, 'ctx', axis=0, tiled=True)]
    pallas_call x0 -> x5, Pallas kernels: none -> 38.1 us  [the longest x2 27.8 us: attend(): pl.pallas_call(attend_kernel, grid=(GROUP,), in_specs=[column(0, True), c...]
    all_to_all x8 -> x3, waiting for transfers between devices: 49.8 us -> 11.9 us  [exchange(): return lax.all_to_all(x, 'head', split_axis=0, concat_axis=0, tiled=True)]
    reduce_sum x28 -> x0, other arithmetic: 19.8 us -> none  [the longest x8 7.68 us: head_terms(): row_dot = jnp.sum(grad_out.astype(jnp.float32) * attended, axis=1)]
    all_to_all x8 -> x3, starting transfers between devices: 28.7 us -> 10.6 us  [exchange(): return lax.all_to_all(x, 'head', split_axis=0, concat_axis=0, tiled=True)]
  transfers between devices with their start and end apart: 12 -> 6, of which waited for: 7 -> 3; matrix products, arithmetic and copies ran while one was open for 6% -> 1% of each run, Pallas kernels for 0% -> 9%
where the time goes in v1:
time: 172 us; the launch traced here: 171 us
  blocking collectives  84.8 us (49%)
  Pallas kernels  38.1 us (22%)
  waiting for transfers between devices  24.8 us (14%)
  starting transfers between devices  15.8 us (9%)
  local copies, waits for them, and re-layouts  5.54 us (3%)
    all_to_all x5, blocking collectives, exchange(): return lax.all_to_all(x, 'head', split_axis=0, concat_axis=0, tiled=True)  61.3 us
    pallas_call x2, Pallas kernels, attend(): pl.pallas_call(attend_kernel, grid=(GROUP,), in_specs=[column(0, True), c...  27.8 us
    all_to_all x1, blocking collectives, shards(): lax.all_to_all(sums.reshape(blocks * parts, 4 * DEPTH), ('ctx', 'head'),...  14.5 us
    all_to_all x3, waiting for transfers between devices, exchange(): return lax.all_to_all(x, 'head', split_axis=0, concat_axis=0, tiled=True)  11.9 us
    all_to_all x3, starting transfers between devices, exchange(): return lax.all_to_all(x, 'head', split_axis=0, concat_axis=0, tiled=True)  10.6 us
    all_to_all x1, blocking collectives, shards(): lax.all_to_all(jnp.concatenate([ds_a, ds_b], axis=1), 'ctx', 0, 0, tiled=...  8.94 us
    ppermute x1, waiting for transfers between devices, shards(): edge_b = lax.ppermute(edge_b, 'ctx', back)  7.86 us
    ppermute x1, waiting for transfers between devices, shards(): edge_a = lax.ppermute(edge_a, 'ctx', back)  5.1 us
  transfers between devices with their start and end apart: 6, of which 3 were waited for; matrix products, arithmetic and copies ran while one was open for 1% of the time, Pallas kernels for 9%

profile of v1, /device:TPU:0, one launch (start us, length us, event | category | flops | bytes accessed | tf_op | source)
XLA Modules:
  0.0 170.6 jit_solution(997584247822422598)
XLA Ops:
  0.6 4.0 %pack.1 = (bf16[4,128,512]{2,1,0:T(8,128)(2,1)}, bf16[4,128,1024]{2,1,0:T(8,128)(2,1)}, bf16[4,128,1024]{2,1,0:T(8,128)(2,1)}, f32[4,1,512]{2,1,0:T(1,128)}) custom-call(bf16[128,4096]{1,0:T(8,128)(2,1)} %q_ref.1, bf16[128,1024]{1,0:T(8,128)(2,1)} %k_ref.1, bf16[128,1024]{1,0:T(8,128)(2,1)} %v_ref.1, bf16[128,4096]{1,0:T(8,128)(2,1)} %g_ref.1), custom_call_target="tpu_custom_call" | custom-call | tf_op jit(solution)/shard_map/pack/pallas_call | solution.py:40
  4.6 0.7 copy.15
  5.3 0.1 all_to_all.39
  5.4 14.5 %all_to_all.60 = f32[32,1,512]{2,1,0:T(1,128)S(1)} all-to-all(f32[32,1,512]{2,1,0:T(1,128)S(1)} %all_to_all.39), channel_id=1, replica_groups=mesh['ctx'=8,'head'=4] {'ctx','head'}, dimensions={0} | all-to-all | bytes 131072 | tf_op jit(solution)/shard_map/all_to_all | solution.py:267
  20.0 12.3 %all_to_all.61 = bf16[4,128,512]{2,1,0:T(8,128)(2,1)S(1)} all-to-all(bf16[4,128,512]{2,1,0:T(8,128)(2,1)} %get-tuple-element.19), channel_id=1, replica_groups=mesh['ctx'=8,'head'=4] {'head'}, dimensions={0} | all-to-all | bytes 1048576 | tf_op jit(solution)/shard_map/all_to_all | solution.py:253
  32.2 0.0 copy-start.3
  32.2 3.5 %all-to-all-start.5 = ((bf16[4,128,1024]{2,1,0:T(8,128)(2,1)}), bf16[4,128,1024]{2,1,0:T(8,128)(2,1)S(1)}, u32[]{:S(2)}, u32[]{:S(2)}) async-start(bf16[4,128,1024]{2,1,0:T(8,128)(2,1)} %get-tuple-element.23), calls=%async_computation.5 | async-start | bytes 2097152 | tf_op jit(solution)/shard_map/all_to_all | solution.py:253
  35.8 0.0 copy-done.3
  35.8 2.5 %collective-permute-start = (bf16[512,512]{1,0:T(8,128)(2,1)S(1)}, bf16[512,512]{1,0:T(8,128)(2,1)S(1)}, u32[]{:S(2)}, u32[]{:S(2)}) collective-permute-start(bf16[512,512]{1,0:T(8,128)(2,1)S(1)} %bitcast.21), channel_id=1, source_target_pairs={{0,4},{4,8},{8,12},{12,16},{16,20},{20,24},{24,28},{1,5},{5,9},{9,... | collective-permute-start | bytes 1572872 | tf_op jit(solution)/shard_map/ppermute | solution.py:265
  38.3 11.8 %all-to-all-done.5 = bf16[4,128,1024]{2,1,0:T(8,128)(2,1)S(1)} async-done(((bf16[4,128,1024]{2,1,0:T(8,128)(2,1)}), bf16[4,128,1024]{2,1,0:T(8,128)(2,1)S(1)}, u32[]{:S(2)}, u32[]{:S(2)}) %all-to-all-start.5) | async-done | bytes 1048608 | tf_op jit(solution)/shard_map/all_to_all | solution.py:253
  50.2 0.0 copy-start.1
  50.2 1.0 copy-done.1
  51.1 3.5 %all-to-all-start = ((bf16[4,128,1024]{2,1,0:T(8,128)(2,1)}), bf16[4,128,1024]{2,1,0:T(8,128)(2,1)S(1)}, u32[]{:S(2)}, u32[]{:S(2)}) async-start(bf16[4,128,1024]{2,1,0:T(8,128)(2,1)} %get-tuple-element.18), calls=%async_computation | async-start | bytes 2097152 | tf_op jit(solution)/shard_map/all_to_all | solution.py:253
  54.7 0.2 reduce
  54.8 0.7 reshape.46.sk_ref.sv_ref
  55.5 0.0 collective-permute-done.pk_ref.pv_ref
  55.5 0.0 copy-start.10
  55.5 0.8 copy-done.10
  56.3 13.9 %attend.3 = (bf16[512,512]{1,0:T(8,128)(2,1)}, bf16[512,512]{1,0:T(8,128)(2,1)}, bf16[512,256]{1,0:T(8,128)(2,1)}, f32[512,256]{1,0:T(8,128)}, f32[8,256]{1,0:T(8,128)}) custom-call(bf16[512,1024]{1,0:T(8,128)(2,1)} %bitcast.17, bf16[512,1024]{1,0:T(8,128)(2,1)} %bitcast.18, bf16[512,512]{1,0:T(8,128)(2,1)} %bitcast.22, bf16[512,512]{1,0:T(8,128)(2,1)} %bitcast.23, ...), custom_call_target="tpu_custom_call" | custom-call | flops 3221225472 | bytes 2097152 | tf_op jit(solution)/shard_map/attend/pallas_call | solution.py:155
  70.1 0.0 all-to-all-done
  70.1 0.0 copy-start.2
  70.2 1.0 copy-done.2
  71.1 0.0 copy-start.9
  71.1 0.0 copy-start.5
  71.1 13.9 %attend.2 = (bf16[512,512]{1,0:T(8,128)(2,1)}, bf16[512,512]{1,0:T(8,128)(2,1)}, bf16[512,256]{1,0:T(8,128)(2,1)}, f32[512,256]{1,0:T(8,128)}, f32[8,256]{1,0:T(8,128)}) custom-call(bf16[512,1024]{1,0:T(8,128)(2,1)} %bitcast.19, bf16[512,1024]{1,0:T(8,128)(2,1)} %bitcast.20, bf16[512,512]{1,0:T(8,128)(2,1)} %bitcast.24, bf16[512,512]{1,0:T(8,128)(2,1)} %bitcast.25, ...), custom_call_target="tpu_custom_call" | custom-call | flops 3221225472 | bytes 2097152 | tf_op jit(solution)/shard_map/attend/pallas_call | solution.py:155
  85.0 0.0 copy-done.9
  85.1 0.7 maximum_bitcast_fusion
  85.8 8.9 %all_to_all.62 = f32[8,1,512]{2,1,0:T(1,128)S(1)} all-to-all(f32[8,1,512]{2,1,0:T(1,128)S(1)} %copy.8), channel_id=1, replica_groups=mesh['ctx'=8,'head'=4] {'ctx'}, dimensions={0} | all-to-all | bytes 32768 | tf_op jit(solution)/shard_map/all_to_all | solution.py:275
  94.7 0.0 copy-done.5
  94.7 0.0 copy-start.4
  94.7 12.1 %all_to_all.63.qb_ref = bf16[4,128,512]{2,1,0:T(8,128)(2,1)} all-to-all(bf16[4,128,512]{2,1,0:T(8,128)(2,1)S(1)} %bitcast.27), channel_id=1, replica_groups=mesh['ctx'=8,'head'=4] {'head'}, dimensions={0} | all-to-all | bytes 1048576 | tf_op jit(solution)/shard_map/all_to_all | solution.py:253
  106.8 0.0 copy-done.4
  106.8 0.0 copy-start.6
  106.8 12.0 %all_to_all.64.ob_ref = bf16[4,128,512]{2,1,0:T(8,128)(2,1)} all-to-all(bf16[4,128,512]{2,1,0:T(8,128)(2,1)S(1)} %bitcast.26), channel_id=1, replica_groups=mesh['ctx'=8,'head'=4] {'head'}, dimensions={0} | all-to-all | bytes 1048576 | tf_op jit(solution)/shard_map/all_to_all | solution.py:253
  118.9 0.0 copy-done.6
  118.9 11.9 %all_to_all.65.qa_ref = bf16[4,128,512]{2,1,0:T(8,128)(2,1)} all-to-all(bf16[4,128,512]{2,1,0:T(8,128)(2,1)S(1)} %bitcast.28), channel_id=1, replica_groups=mesh['ctx'=8,'head'=4] {'head'}, dimensions={0} | all-to-all | bytes 1048576 | tf_op jit(solution)/shard_map/all_to_all | solution.py:253
  130.8 0.0 copy-start.11
  130.8 0.0 copy-start.12
  130.8 3.6 %all-to-all-start.3 = ((bf16[4,128,512]{2,1,0:T(8,128)(2,1)}), bf16[4,128,512]{2,1,0:T(8,128)(2,1)S(1)}, u32[]{:S(2)}, u32[]{:S(2)}) async-start(bf16[4,128,512]{2,1,0:T(8,128)(2,1)} %bitcast.2), calls=%async_computation.3 | async-start | bytes 1048576 | tf_op jit(solution)/shard_map/all_to_all | solution.py:253
  134.4 0.0 copy-done.11
  134.4 1.3 collective-permute-start.2
  135.7 0.0 copy-done.12
  135.7 1.3 collective-permute-start.1
  137.0 0.6 copy.14
  137.6 7.9 %collective-permute-done.2.edge_b = bf16[512,256]{1,0:T(8,128)(2,1)S(1)} collective-permute-done((bf16[512,256]{1,0:T(8,128)(2,1)S(1)}, bf16[512,256]{1,0:T(8,128)(2,1)S(1)}, u32[]{:S(2)}, u32[]{:S(2)}) %collective-permute-start.2) | collective-permute-done | bytes 262176 | tf_op jit(solution)/shard_map/ppermute | solution.py:274
  145.5 0.0 copy-start.7
  145.5 5.1 %collective-permute-done.1.edge_a = bf16[512,256]{1,0:T(8,128)(2,1)S(1)} collective-permute-done((bf16[512,256]{1,0:T(8,128)(2,1)S(1)}, bf16[512,256]{1,0:T(8,128)(2,1)S(1)}, u32[]{:S(2)}, u32[]{:S(2)}) %collective-permute-start.1) | collective-permute-done | bytes 262176 | tf_op jit(solution)/shard_map/ppermute | solution.py:273
  150.6 0.0 copy-start.8
  150.6 0.0 copy-done.7
  150.6 0.7 copy-done.8
  151.3 2.3 %join.1 = bf16[512,512]{1,0:T(8,128)(2,1)} custom-call(f32[512,256]{1,0:T(8,128)} %get-tuple-element.26.own_a, f32[512,256]{1,0:T(8,128)} %get-tuple-element.27.own_b, bf16[512,256]{1,0:T(8,128)(2,1)} %copy-done.8, bf16[512,256]{1,0:T(8,128)(2,1)} %copy-done.7, f32[8,512]{1,0:T(8,128)} %bitcast.29), custom_call_target="tpu_custom_call" | custom-call | tf_op jit(solution)/shard_map/join/pallas_call | solution.py:212
  153.6 0.0 all-to-all-done.3.oa_ref
  153.6 0.0 copy-start
  153.6 13.0 %all_to_all.66.kv_ref = bf16[4,128,512]{2,1,0:T(8,128)(2,1)} all-to-all(bf16[4,128,512]{2,1,0:T(8,128)(2,1)} %bitcast.16), channel_id=1, replica_groups=mesh['ctx'=8,'head'=4] {'head'}, dimensions={0} | all-to-all | bytes 1048576 | tf_op jit(solution)/shard_map/all_to_all | solution.py:253
  166.6 0.0 copy-done
  166.6 4.0 %unpack.1 = (bf16[128,4096]{1,0:T(8,128)(2,1)}, bf16[128,4096]{1,0:T(8,128)(2,1)}, bf16[128,1024]{1,0:T(8,128)(2,1)}, bf16[128,1024]{1,0:T(8,128)(2,1)}) custom-call(bf16[4,128,512]{2,1,0:T(8,128)(2,1)} %copy-done, bf16[4,128,512]{2,1,0:T(8,128)(2,1)} %all_to_all.65.qa_ref, bf16[4,128,512]{2,1,0:T(8,128)(2,1)} %all_to_all.64.ob_ref, ...), custom_call_target="tpu_custom_call" | custom-call | tf_op jit(solution)/shard_map/unpack/pallas_call | solution.py:232
  (2 shorter events, 0.0 us)
Async XLA Ops:
  32.2 3.5 %copy-start.3 = (bf16[4,128,512]{2,1,0:T(8,128)(2,1)}, bf16[4,128,512]{2,1,0:T(8,128)(2,1)S(1)}, u32[]{:S(2)}) copy-start(bf16[4,128,512]{2,1,0:T(8,128)(2,1)S(1)} %all_to_all.61) | copy-start | bytes 1572868
  32.2 17.9 %all-to-all-start.5 = ((bf16[4,128,1024]{2,1,0:T(8,128)(2,1)}), bf16[4,128,1024]{2,1,0:T(8,128)(2,1)S(1)}, u32[]{:S(2)}, u32[]{:S(2)}) async-start(bf16[4,128,1024]{2,1,0:T(8,128)(2,1)} %get-tuple-element.23), calls=%async_computation.5 | async-start | bytes 2097152 | tf_op jit(solution)/shard_map/all_to_all | solution.py:253
  35.8 19.7 %collective-permute-start = (bf16[512,512]{1,0:T(8,128)(2,1)S(1)}, bf16[512,512]{1,0:T(8,128)(2,1)S(1)}, u32[]{:S(2)}, u32[]{:S(2)}) collective-permute-start(bf16[512,512]{1,0:T(8,128)(2,1)S(1)} %bitcast.21), channel_id=1, source_target_pairs={{0,4},{4,8},{8,12},{12,16},{16,20},{20,24},{24,28},{1,5},{5,9},{9,... | collective-permute-start | bytes 1572872 | tf_op jit(solution)/shard_map/ppermute | solution.py:265
  50.2 1.0 copy-start.1
  51.1 19.0 %all-to-all-start = ((bf16[4,128,1024]{2,1,0:T(8,128)(2,1)}), bf16[4,128,1024]{2,1,0:T(8,128)(2,1)S(1)}, u32[]{:S(2)}, u32[]{:S(2)}) async-start(bf16[4,128,1024]{2,1,0:T(8,128)(2,1)} %get-tuple-element.18), calls=%async_computation | async-start | bytes 2097152 | tf_op jit(solution)/shard_map/all_to_all | solution.py:253
  55.5 0.8 copy-start.10
  70.1 1.0 copy-start.2
  71.1 13.9 %copy-start.9 = (f32[8,256]{1,0:T(8,128)S(1)}, f32[8,256]{1,0:T(8,128)}, u32[]{:S(2)}) copy-start(f32[8,256]{1,0:T(8,128)} %get-tuple-element.31) | copy-start | bytes 24580
  71.1 23.6 %copy-start.5 = (bf16[512,512]{1,0:T(8,128)(2,1)S(1)}, bf16[512,512]{1,0:T(8,128)(2,1)}, u32[]{:S(2)}) copy-start(bf16[512,512]{1,0:T(8,128)(2,1)} %get-tuple-element.25) | copy-start | bytes 1572868
  94.7 12.1 %copy-start.4 = (bf16[512,512]{1,0:T(8,128)(2,1)S(1)}, bf16[512,512]{1,0:T(8,128)(2,1)}, u32[]{:S(2)}) copy-start(bf16[512,512]{1,0:T(8,128)(2,1)} %get-tuple-element.24) | copy-start | bytes 1572868
  106.8 12.0 %copy-start.6 = (bf16[512,512]{1,0:T(8,128)(2,1)S(1)}, bf16[512,512]{1,0:T(8,128)(2,1)}, u32[]{:S(2)}) copy-start(bf16[512,512]{1,0:T(8,128)(2,1)} %get-tuple-element.22) | copy-start | bytes 1572868
  130.8 3.6 %copy-start.11 = (bf16[512,256]{1,0:T(8,128)(2,1)S(1)}, bf16[512,256]{1,0:T(8,128)(2,1)}, u32[]{:S(2)}) copy-start(bf16[512,256]{1,0:T(8,128)(2,1)} %get-tuple-element.29) | copy-start | bytes 786436
  130.8 4.9 %copy-start.12 = (bf16[512,256]{1,0:T(8,128)(2,1)S(1)}, bf16[512,256]{1,0:T(8,128)(2,1)}, u32[]{:S(2)}) copy-start(bf16[512,256]{1,0:T(8,128)(2,1)} %get-tuple-element.28) | copy-start | bytes 786436
  130.8 22.8 %all-to-all-start.3 = ((bf16[4,128,512]{2,1,0:T(8,128)(2,1)}), bf16[4,128,512]{2,1,0:T(8,128)(2,1)S(1)}, u32[]{:S(2)}, u32[]{:S(2)}) async-start(bf16[4,128,512]{2,1,0:T(8,128)(2,1)} %bitcast.2), calls=%async_computation.3 | async-start | bytes 1048576 | tf_op jit(solution)/shard_map/all_to_all | solution.py:253
  134.4 11.1 %collective-permute-start.2 = (bf16[512,256]{1,0:T(8,128)(2,1)S(1)}, bf16[512,256]{1,0:T(8,128)(2,1)S(1)}, u32[]{:S(2)}, u32[]{:S(2)}) collective-permute-start(bf16[512,256]{1,0:T(8,128)(2,1)S(1)} %copy-done.11), channel_id=1, source_target_pairs={{4,0},{8,4},{12,8},{16,12},{20,16},{24,20},{28,24},{5,1},{9,5},{13... | collective-permute-start | bytes 786440 | tf_op jit(solution)/shard_map/ppermute | solution.py:274
  135.7 14.9 %collective-permute-start.1 = (bf16[512,256]{1,0:T(8,128)(2,1)S(1)}, bf16[512,256]{1,0:T(8,128)(2,1)S(1)}, u32[]{:S(2)}, u32[]{:S(2)}) collective-permute-start(bf16[512,256]{1,0:T(8,128)(2,1)S(1)} %copy-done.12), channel_id=1, source_target_pairs={{4,0},{8,4},{12,8},{16,12},{20,16},{24,20},{28,24},{5,1},{9,5},{13... | collective-permute-start | bytes 786440 | tf_op jit(solution)/shard_map/ppermute | solution.py:273
  145.5 5.1 %copy-start.7 = (bf16[512,256]{1,0:T(8,128)(2,1)}, bf16[512,256]{1,0:T(8,128)(2,1)S(1)}, u32[]{:S(2)}) copy-start(bf16[512,256]{1,0:T(8,128)(2,1)S(1)} %collective-permute-done.2.edge_b) | copy-start | bytes 786436
  150.6 0.7 copy-start.8
  153.6 13.0 %copy-start = (bf16[4,128,512]{2,1,0:T(8,128)(2,1)}, bf16[4,128,512]{2,1,0:T(8,128)(2,1)S(1)}, u32[]{:S(2)}) copy-start(bf16[4,128,512]{2,1,0:T(8,128)(2,1)S(1)} %all-to-all-done.3.oa_ref) | copy-start | bytes 1572868
